TPU v7x, 128 devices: a whole 4x4x4 slice. The times are simulated.
128 devices in a mesh: group: 4 (over x), bulk: 32 (over z, y, core).
Axes of the slice: x: 4, y: 4, z: 4, core: 2. Of those that a mesh axis runs over, the one named last changes fastest.
Arguments:
- rhs: float32 [512, 64, 128], P(('group', 'bulk')), may hold values from -90 to 90, as said below
- diag_tiles: float32 [512, 128, 128], P(('group', 'bulk')), may hold values from -0.06 to 0.06
- offdiag_blocks: float32 [512, 11, 128, 128], P(('group', 'bulk')), may hold values from -0.026 to 0.026
- coupling: float32 [256, 4, 128, 128], P(('group', 'bulk')), may hold values from -0.05 to 0.05, as said below
- col_index: int32 [512, 11], replicated, may hold values from 0 to 511, as said below
- load: int32 [512], replicated, may hold values from 3 to 11
- new_slot: int32 [512], replicated, may hold values from 0 to 511, as said below
Outputs:
- solution_out: float32 [512, 64, 128], P(('group', 'bulk'))
- residual_out: float32 [512, 64, 128], P(('group', 'bulk'))
Inputs may be any that keep to these rules, and one draw needn't show every extreme that they name: `rhs`: made of random entries times scales of the rows and of the columns. `coupling`: entry [d * 2 + k, h] is the transpose of entry [(h * 32 + d % 32) * 2 + k, d // 32]. `col_index`: for each part g and each tile position t, the column t of the 128 block rows of part g is a permutation of that part's slots g * 128 to (g + 1) * 128 - 1. Of the 44 entries of the 4 block rows of one device (slots d * 4 to (d + 1) * 4 - 1), at most 2 name slots of any one device, and exactly 2 name slots of some device. `new_slot`: A permutation. On every device exactly one block row moves, from a slot k with 2 <= k % 4; it stays in its part, goes from owner b to owner b XOR m, where m (1 to 31) is one number for the whole part, and takes the slot that the moving row of that device leaves.
All inputs are finite; a program needn't handle non-finite values.
Results may differ from a plain program's by a relative error of at most 0.0003.
Values sent between devices are 32-bit elements; how exact they have to be, the bound alone decides.
A program may use at most 64 MiB of HBM per device.

v0:
```python
import jax
import jax.numpy as jnp
from jax import lax
from jax.sharding import PartitionSpec as P

highest = lax.Precision.HIGHEST
diagonal_shift = 4.0


def from_partner(value, axis, bit):
    mask = 2**bit
    pairs = [(source, source ^ mask) for source in range(lax.axis_size(axis))]
    return lax.ppermute(value, axis, pairs)


def chol_apply(matrix, right):
    factor = jnp.linalg.cholesky(matrix)
    middle = lax.linalg.triangular_solve(factor, right, left_side=True, lower=True)
    return lax.linalg.triangular_solve(factor, middle, left_side=True, lower=True, transpose_a=True)


def global_gram(left, right):
    partial_gram = jnp.einsum("snt,smt->nm", left, right, precision=highest)
    total = lax.psum(partial_gram, ("group", "bulk"))
    return 0.5 * (total + total.T)


def operate(vectors, diag, masked, column_ids, coupling):
    row_count = vectors.shape[0]
    boundary_rows = coupling.shape[0]
    part_count = coupling.shape[1]
    group_rows = row_count * lax.axis_size("bulk")
    border = lax.all_gather(vectors[:boundary_rows], "group", axis=0, tiled=True)
    final_output = diagonal_shift * vectors + jnp.einsum(
        "rnj,rij->rni", vectors, diag, precision=highest
    )
    returned = jnp.einsum("rni,rkij->rknj", vectors, masked, precision=highest)
    flat_terms = returned.reshape((-1,) + vectors.shape[1:])
    panel = lax.all_gather(vectors, "bulk", axis=0, tiled=True)
    buffer = jax.ops.segment_sum(flat_terms, column_ids.reshape(-1), num_segments=group_rows)
    owed = lax.psum_scatter(buffer, "bulk", scatter_dimension=0, tiled=True)
    picked = panel[column_ids]
    final_output = (
        final_output + jnp.einsum("rknj,rkij->rni", picked, masked, precision=highest) + owed
    )
    border = border.reshape((part_count, boundary_rows) + vectors.shape[1:])
    crossed = jnp.einsum("khij,hknj->kni", coupling, border, precision=highest)
    return final_output.at[:boundary_rows].add(crossed)


def advance(state, diag, masked, column_ids, coupling, last_step):
    solution, resid, direction, gram_rr = state
    image = operate(direction, diag, masked, column_ids, coupling)
    gram_pq = global_gram(direction, image)
    alpha = chol_apply(gram_pq, gram_rr)
    solution = solution + jnp.einsum("mn,smt->snt", alpha, direction, precision=highest)
    resid = resid - jnp.einsum("mn,smt->snt", alpha, image, precision=highest)
    if not last_step:
        gram_new = global_gram(resid, resid)
        beta = chol_apply(gram_rr, gram_new)
        direction = resid + jnp.einsum("mn,smt->snt", beta, direction, precision=highest)
        gram_rr = gram_new
    return (solution, resid, direction, gram_rr)


def local(rhs, diag_tiles, offdiag_blocks, coupling, col_index, load, new_slot):
    row_count = rhs.shape[0]
    off_count = offdiag_blocks.shape[1]
    bulk_count = lax.axis_size("bulk")
    group_rows = row_count * bulk_count
    my_group = lax.axis_index("group")
    my_bulk = lax.axis_index("bulk")
    first_slot = (my_group * bulk_count + my_bulk) * row_count
    group_base = my_group * group_rows
    own_slots = first_slot + jnp.arange(row_count, dtype=jnp.int32)
    tile_ids = jnp.arange(off_count, dtype=jnp.int32)
    old_columns = col_index[own_slots] - group_base
    old_mask = (tile_ids[None, :] < load[own_slots][:, None]).astype(jnp.float32)
    old_masked = offdiag_blocks * old_mask[:, :, None, None]
    own_new = new_slot[own_slots]
    leaving = jnp.argmax((own_new != own_slots).astype(jnp.int32))
    target = own_new[leaving]
    target_bulk = target // row_count % bulk_count
    xor_mask = jnp.bitwise_xor(target_bulk, my_bulk)
    start_state = (jnp.zeros_like(rhs), rhs, rhs, global_gram(rhs, rhs))
    state = advance(start_state, diag_tiles, old_masked, old_columns, coupling, False)
    solution, resid, direction, gram_rr = state
    pieces = [
        offdiag_blocks[leaving],
        diag_tiles[leaving],
        solution[leaving],
        resid[leaving],
        direction[leaving],
    ]
    flat = jnp.concatenate([piece.reshape(-1) for piece in pieces])
    for bit_pos in range(bulk_count.bit_length() - 1):
        partner = from_partner(flat, "bulk", bit_pos)
        chosen = jnp.bitwise_and(jnp.right_shift(xor_mask, bit_pos), 1) == 1
        flat = jnp.where(chosen, partner, flat)
    outputs = []
    offset = 0
    for piece in pieces:
        outputs.append(flat[offset : offset + piece.size].reshape(piece.shape))
        offset = offset + piece.size
    moved_off = offdiag_blocks.at[leaving].set(outputs[0])
    moved_diag = diag_tiles.at[leaving].set(outputs[1])
    solution = solution.at[leaving].set(outputs[2])
    resid = resid.at[leaving].set(outputs[3])
    direction = direction.at[leaving].set(outputs[4])
    inverse = (
        jnp.zeros_like(new_slot).at[new_slot].set(jnp.arange(new_slot.shape[0], dtype=jnp.int32))
    )
    old_rows = inverse[own_slots]
    new_columns = new_slot[col_index[old_rows]] - group_base
    new_mask = (tile_ids[None, :] < load[old_rows][:, None]).astype(jnp.float32)
    new_masked = moved_off * new_mask[:, :, None, None]
    state = advance(
        (solution, resid, direction, gram_rr), moved_diag, new_masked, new_columns, coupling, True
    )
    return (state[0], state[1])


def solution(mesh):
    return jax.shard_map(
        local,
        mesh=mesh,
        in_specs=(
            P(("group", "bulk"), None, None),
            P(("group", "bulk"), None, None),
            P(("group", "bulk"), None, None, None),
            P(("group", "bulk"), None, None, None),
            P(),
            P(),
            P(),
        ),
        out_specs=(P(("group", "bulk"), None, None), P(("group", "bulk"), None, None)),
        check_vma=False,
    )
```

profile of v0, /device:TPU:1, one launch (start us, length us, event | category | flops | bytes accessed | tf_op | source)
XLA Modules:
  0.0 662.4 jit_solution(1041182074401895514)
XLA Ops:
  7.3 1.9 copy.86
  9.9 1.6 copy.40
  12.1 2.6 scatter_custom_fusion.1
  15.9 1.5 gather_fusion
  18.7 2.2 gather_fusion.5
  25.3 3.2 fusion.4
  28.5 2.5 broadcast.320.clone
  31.0 8.0 %scatter_fusion = f32[128,64,128]{2,1,0:T(8,128)} fusion(f32[128,64,128]{2,1,0:T(8,128)} %broadcast.320.clone, s32[44]{0:T(128)} %reshape.516, f32[44,64,128]{2,1,0:T(8,128)} %bitcast.222), kind=kCustom, calls=%fused_computation.9 | custom fusion | flops 360448 | bytes 4325552 | tf_op jit(solution)/shard_map/scatter-add | solution.py:40
  40.2 1.3 fusion.68
  45.5 13.0 %all_gather.13 = f32[8,64,128]{2,1,0:T(8,128)} all-gather(f32[2,64,128]{2,1,0:T(8,128)} %slice.208), channel_id=1, replica_groups=mesh['group'=4,'bulk'=32] {'group'}, dimensions={0}, use_global_device_ids=true | all-gather | bytes 327680 | tf_op jit(solution)/shard_map/all_gather | solution.py:33
  60.9 1.5 bitcast_dynamic-update-slice_fusion
  62.4 4.0 gather_fusion.1
  66.4 5.4 fusion.12
  71.8 71.6 %reduce-scatter.3.cloned.1.call-done = f32[4,64,128]{2,1,0:T(8,128)} async-done(((f32[128,64,128]{2,1,0:T(8,128)}), f32[4,64,128]{2,1,0:T(8,128)}) %reduce-scatter.3.cloned.1.call-update) | async-done | bytes 131088 | tf_op jit(solution)/shard_map/reduce_scatter | solution.py:41
  143.4 1.7 fusion.21
  145.1 1.6 fusion.29
  148.2 66.3 %all-reduce = (f32[64,64]{1,0:T(8,128)}, f32[64,64]{1,0:T(8,128)}) all-reduce(f32[64,64]{1,0:T(8,128)} %convolution_bitcast_fusion.11, f32[64,64]{1,0:T(8,128)} %convolution_bitcast_fusion.12), channel_id=1, replica_groups=mesh['group'=4,'bulk'=32] {'group','bulk'}, use_global_device_ids=true, to_apply=%region_5.7 | all-reduce | flops 8192 | bytes 65536 | tf_op jit(solution)/shard_map/psum | solution.py:24
  214.6 1.4 copy.45
  216.0 1.4 fusion.56
  217.4 1.4 copy.48
  218.8 1.5 copy.43
  220.3 1.4 fusion.61
  221.7 1.4 copy.44
  223.1 1.4 fusion.60
  224.5 7.2 %cholesky.59 = f32[64,64]{1,0:T(8,128)} custom-call(f32[64,64]{1,0:T(8,128)} %fusion.60), custom_call_target="Cholesky" | custom-call | tf_op jit(solution)/shard_map/jit(cholesky)/cholesky | solution.py:17
  233.2 2.1 fusion.36
  235.3 6.3 custom-call.13
  243.6 1.8 fusion.25
  246.3 1.4 fusion.55
  247.7 7.2 %cholesky.70 = f32[64,64]{1,0:T(8,128)} custom-call(f32[64,64]{1,0:T(8,128)} %fusion.55), custom_call_target="Cholesky" | custom-call | tf_op jit(solution)/shard_map/jit(cholesky)/cholesky | solution.py:17
  256.4 2.1 fusion.37
  258.5 6.3 custom-call.15
  264.7 1.8 convolution_bitcast_fusion.9
  266.6 63.0 %psum.30 = f32[64,64]{1,0:T(8,128)} all-reduce(f32[64,64]{1,0:T(8,128)} %convolution_bitcast_fusion.9), channel_id=1, replica_groups=mesh['group'=4,'bulk'=32] {'group','bulk'}, use_global_device_ids=true, to_apply=%region_8.12 | all-reduce | flops 4096 | bytes 32768 | tf_op jit(solution)/shard_map/psum | solution.py:24
  329.6 1.4 copy.49
  334.2 1.4 bitcast_dynamic-update-slice_fusion.3
  335.6 1.4 bitcast_dynamic-update-slice_fusion.2
  341.3 2.2 broadcast_select_fusion
  344.7 20.3 %collective-permute-done.1 = f32[221184]{0:T(1024)} collective-permute-done((f32[221184]{0:T(1024)}, f32[221184]{0:T(1024)}, u32[]{:S(2)}, u32[]{:S(2)}) %collective-permute-start.1) | collective-permute-done | bytes 884768 | tf_op jit(solution)/shard_map/ppermute | solution.py:13
  365.0 2.2 broadcast_select_fusion.1
  367.2 2.9 collective-permute-start.2
  370.2 19.2 %collective-permute-done.2 = f32[221184]{0:T(1024)} collective-permute-done((f32[221184]{0:T(1024)}, f32[221184]{0:T(1024)}, u32[]{:S(2)}, u32[]{:S(2)}) %collective-permute-start.2) | collective-permute-done | bytes 884768 | tf_op jit(solution)/shard_map/ppermute | solution.py:13
  389.4 2.2 broadcast_select_fusion.2
  392.7 18.7 %collective-permute-done.3 = f32[221184]{0:T(1024)} collective-permute-done((f32[221184]{0:T(1024)}, f32[221184]{0:T(1024)}, u32[]{:S(2)}, u32[]{:S(2)}) %collective-permute-start.3) | collective-permute-done | bytes 884768 | tf_op jit(solution)/shard_map/ppermute | solution.py:13
  411.4 2.2 broadcast_select_fusion.3
  413.6 2.3 collective-permute-start.4
  416.7 17.4 %collective-permute-done.4 = f32[221184]{0:T(1024)} collective-permute-done((f32[221184]{0:T(1024)}, f32[221184]{0:T(1024)}, u32[]{:S(2)}, u32[]{:S(2)}) %collective-permute-start.4) | collective-permute-done | bytes 884768 | tf_op jit(solution)/shard_map/ppermute | solution.py:13
  436.2 2.0 fusion.40
  441.4 1.4 and_reduce_fusion
  445.4 3.2 fusion
  448.6 2.5 broadcast.320
  451.1 7.8 %scatter_fusion.1 = f32[128,64,128]{2,1,0:T(8,128)} fusion(f32[128,64,128]{2,1,0:T(8,128)} %broadcast.320, s32[44]{0:T(128)S(1)} %broadcast_subtract_fusion.1, f32[44,64,128]{2,1,0:T(8,128)} %bitcast.223), kind=kCustom, calls=%fused_computation.11 | custom fusion | flops 360448 | bytes 4325552 | tf_op jit(solution)/shard_map/scatter-add | solution.py:40
  459.2 10.1 %all_gather.15 = f32[8,64,128]{2,1,0:T(8,128)} all-gather(f32[2,64,128]{2,1,0:T(8,128)S(1)} %slice.243), channel_id=1, replica_groups=mesh['group'=4,'bulk'=32] {'group'}, dimensions={0}, use_global_device_ids=true | all-gather | bytes 327680 | tf_op jit(solution)/shard_map/all_gather | solution.py:33
  469.3 2.1 fusion.35
  471.4 15.3 %all-gather.5.cloned.1.call-done = f32[128,64,128]{2,1,0:T(8,128)} async-done(((f32[4,64,128]{2,1,0:T(8,128)}), f32[128,64,128]{2,1,0:T(8,128)}) %all-gather.5.cloned.1.call-update) | async-done | bytes 4194320 | tf_op jit(solution)/shard_map/all_gather | solution.py:39
  486.7 4.0 gather_fusion.7
  490.7 5.4 fusion.15
  496.2 73.8 %reduce-scatter.5.cloned.1.call-done = f32[4,64,128]{2,1,0:T(8,128)} async-done(((f32[128,64,128]{2,1,0:T(8,128)}), f32[4,64,128]{2,1,0:T(8,128)}) %reduce-scatter.5.cloned.1.call-update) | async-done | bytes 131088 | tf_op jit(solution)/shard_map/reduce_scatter | solution.py:41
  570.0 1.7 fusion.19
  571.6 1.6 fusion.27
  573.5 66.0 %psum.31 = f32[64,64]{1,0:T(8,128)S(1)} all-reduce(f32[64,64]{1,0:T(8,128)S(1)} %convolution_bitcast_fusion.7), channel_id=1, replica_groups=mesh['group'=4,'bulk'=32] {'group','bulk'}, use_global_device_ids=true, to_apply=%region_13.17 | all-reduce | flops 4096 | bytes 32768 | tf_op jit(solution)/shard_map/psum | solution.py:24
  639.7 5.8 cholesky.81
  646.9 4.9 custom-call.17
  653.1 1.8 fusion.22
  (102 shorter events, 41.5 us)
Async XLA Ops:
  7.2 137.9 %copy-start = (f32[2,4,128,128]{3,2,1,0:T(8,128)S(1)}, f32[2,4,128,128]{3,2,1,0:T(8,128)}, u32[]{:S(2)}) copy-start(f32[2,4,128,128]{3,2,1,0:T(8,128)} %param.29) | copy-start | bytes 1572868
  7.2 18.1 %copy-start.3 = (f32[4,64,128]{2,1,0:T(8,128)S(1)}, f32[4,64,128]{2,1,0:T(8,128)}, u32[]{:S(2)}) copy-start(f32[4,64,128]{2,1,0:T(8,128)} %param.26) | copy-start | bytes 393220
  7.2 16.2 %copy-start.2 = (s32[512]{0:T(512)S(1)}, s32[512]{0:T(512)}, u32[]{:S(2)}) copy-start(s32[512]{0:T(512)} %param.31) | copy-start | bytes 6148
  7.2 4.3 copy-start.1
  7.2 55.2 %all-gather.3.cloned.1.call-start = ((), (), s32[]{:S(2)}) async-start(), calls=%async_computation.2 | async-start | bytes 4325376 | tf_op jit(solution)/shard_map/all_gather | solution.py:39
  7.3 1.9 copy-start.11
  9.9 133.5 %reduce-scatter.3.cloned.1.call-start = ((), (), s32[]{:S(2)}) async-start(), calls=%async_computation.3 | async-start | bytes 4325376 | tf_op jit(solution)/shard_map/reduce_scatter | solution.py:41
  39.0 447.7 %all-gather.5.cloned.1.call-start = ((), (), s32[]{:S(2)}) async-start(), calls=%async_computation.4 | async-start | bytes 4325376 | tf_op jit(solution)/shard_map/all_gather | solution.py:39
  71.8 266.4 %copy-start.13 = (s32[4]{0:T(128)S(1)}, s32[4]{0:T(128)}, u32[]{:S(2)}) copy-start(s32[4]{0:T(128)} %gather_fusion.3) | copy-start | bytes 52
  146.7 0.7 copy-start.7
  334.2 2.8 copy-start.4
  337.6 3.7 collective-permute-start
  343.5 21.5 %collective-permute-start.1 = (f32[221184]{0:T(1024)}, f32[221184]{0:T(1024)}, u32[]{:S(2)}, u32[]{:S(2)}) collective-permute-start(f32[221184]{0:T(1024)} %broadcast_select_fusion), channel_id=1, source_target_pairs={{0,2},{1,3},{2,0},{3,1},{4,6},{5,7},{6,4},{7,5},{8,10},{9,11},{10,... | collective-permute-start | bytes 2654216 | tf_op jit(solution)/shard_map/ppermute | solution.py:13
  367.2 48.7 %copy-start.14 = (s32[3]{0:T(128)S(1)}, s32[3]{0:T(128)}, u32[]{:S(2)}) copy-start(s32[3]{0:T(128)} %constant.237.clone.1) | copy-start | bytes 40
  367.2 49.5 %copy-start.8 = (f32[64,4,128]{2,0,1:T(8,128)S(1)}, f32[64,4,128]{2,0,1:T(8,128)}, u32[]{:S(2)}) copy-start(f32[64,4,128]{2,0,1:T(8,128)} %fusion.73) | copy-start | bytes 393220
  367.2 22.2 %collective-permute-start.2 = (f32[221184]{0:T(1024)}, f32[221184]{0:T(1024)}, u32[]{:S(2)}, u32[]{:S(2)}) collective-permute-start(f32[221184]{0:T(1024)} %broadcast_select_fusion.1), channel_id=1, source_target_pairs={{0,4},{1,5},{2,6},{3,7},{4,0},{5,1},{6,2},{7,3},{8,12},{9,13},{10,... | collective-permute-start | bytes 2654216 | tf_op jit(solution)/shard_map/ppermute | solution.py:13
  391.6 19.8 %collective-permute-start.3 = (f32[221184]{0:T(1024)}, f32[221184]{0:T(1024)}, u32[]{:S(2)}, u32[]{:S(2)}) collective-permute-start(f32[221184]{0:T(1024)} %broadcast_select_fusion.2), channel_id=1, source_target_pairs={{0,8},{1,9},{2,10},{3,11},{4,12},{5,13},{6,14},{7,15},{8,0},{9,1},... | collective-permute-start | bytes 2654216 | tf_op jit(solution)/shard_map/ppermute | solution.py:13
  392.7 47.8 %copy-start.12 = (s32[4,11,1]{1,0,2:T(4,128)S(1)}, s32[4,11,1]{1,0,2:T(4,128)}, u32[]{:S(2)}) copy-start(s32[4,11,1]{1,0,2:T(4,128)} %get-tuple-element.98) | copy-start | bytes 532
  413.6 20.5 %collective-permute-start.4 = (f32[221184]{0:T(1024)}, f32[221184]{0:T(1024)}, u32[]{:S(2)}, u32[]{:S(2)}) collective-permute-start(f32[221184]{0:T(1024)} %broadcast_select_fusion.3), channel_id=1, source_target_pairs={{0,16},{1,17},{2,18},{3,19},{4,20},{5,21},{6,22},{7,23},{8,24},{9,... | collective-permute-start | bytes 2654216 | tf_op jit(solution)/shard_map/ppermute | solution.py:13
  435.3 0.9 copy-start.6
  438.3 0.7 copy-start.9
  438.9 131.0 %reduce-scatter.5.cloned.1.call-start = ((), (), s32[]{:S(2)}) async-start(), calls=%async_computation.5 | async-start | bytes 4325376 | tf_op jit(solution)/shard_map/reduce_scatter | solution.py:41
  440.5 4.9 copy-start.5
  496.2 158.8 %copy-start.10 = (f32[4,64,128]{2,1,0:T(8,128)S(1)}, f32[4,64,128]{2,1,0:T(8,128)}, u32[]{:S(2)}) copy-start(f32[4,64,128]{2,1,0:T(8,128)} %copy-done.9) | copy-start | bytes 393220
Sparse Core Ops, SparseCore 0:
  10.3 49.7 all-gather.2
  63.7 79.6 reduce-scatter.2
  439.1 47.6 all-gather.4
  490.2 79.7 reduce-scatter.4
where the time goes:
time: 666 us; the launch traced here: 662 us
  waiting for transfers between devices  236 us (35%)
  blocking collectives  218 us (33%)
  other arithmetic  90.6 us (14%)
  local copies, waits for them, and re-layouts  50.3 us (8%)
  matrix products  39.5 us (6%)
  between operations  18.6 us (3%)
  starting transfers between devices  8.54 us (1%)
    psum x3, blocking collectives, global_gram(): total = lax.psum(partial_gram, ('group', 'bulk'))  195 us
    reduce_scatter x2, waiting for transfers between devices, operate(): owed = lax.psum_scatter(buffer, 'bulk', scatter_dimension=0, tiled=True)  145 us
    ppermute x5, waiting for transfers between devices, from_partner(): return lax.ppermute(value, axis, pairs)  75.6 us
    another operation x9, other arithmetic, chol_apply(): factor = jnp.linalg.cholesky(matrix)  23.9 us
    all_gather x2, blocking collectives, operate(): lax.all_gather(vectors[:boundary_rows], 'group', axis=0, tiled=True)  23.1 us
    another operation x6, other arithmetic, chol_apply(): lax.linalg.triangular_solve(factor, middle, left_side=True, lower=True, t...  22.2 us
    scatter-add x2, other arithmetic, operate(): jax.ops.segment_sum(flat_terms, column_ids.reshape(-1), num_segments=grou...  15.8 us
    all_gather x2, waiting for transfers between devices, operate(): panel = lax.all_gather(vectors, 'bulk', axis=0, tiled=True)  15.3 us
  transfers between devices with their start and end apart: 9, of which 7 were waited for; matrix products, arithmetic and copies ran while one was open for 12% of the time, Pallas kernels for 0%

commit v1 on v0

--- a/solution.py
+++ b/solution.py
@@ -21,7 +21,7 @@
 
 def global_gram(left, right):
     partial_gram = jnp.einsum("snt,smt->nm", left, right, precision=highest)
-    total = lax.psum(partial_gram, ("group", "bulk"))
+    total = jnp.sum(lax.all_gather(partial_gram, ("group", "bulk")), axis=0)
     return 0.5 * (total + total.T)
 
 

time: 666 us -> 717 us (1.077)
  waiting for transfers between devices: 236 us -> 477 us
  blocking collectives: 218 us -> 23.3 us
  other arithmetic: 90.6 us -> 102 us
    all_gather x0 -> x4, waiting for transfers between devices: none -> 229 us  [global_gram(): total = jnp.sum(lax.all_gather(partial_gram, ('group', 'bulk')), axis=0)]
    psum x3 -> x0, blocking collectives: 195 us -> none  [global_gram(): total = lax.psum(partial_gram, ('group', 'bulk'))]
    reduce_sum x0 -> x4, other arithmetic: none -> 11.9 us  [global_gram(): total = jnp.sum(lax.all_gather(partial_gram, ('group', 'bulk')), axis=0)]
    unnamed x38 -> x53, local copies, waits for them, and re-layouts: 11.6 us -> 14.8 us
  transfers between devices with their start and end apart: 9 -> 13, of which waited for: 7 -> 12; matrix products, arithmetic and copies ran while one was open for 12% -> 16% of each run, Pallas kernels for 0% -> 0%
where the time goes in v1:
time: 717 us; the launch traced here: 714 us
  waiting for transfers between devices  477 us (67%)
  other arithmetic  102 us (14%)
  local copies, waits for them, and re-layouts  52.3 us (7%)
  matrix products  36.8 us (5%)
  blocking collectives  23.3 us (3%)
  between operations  19 us (3%)
    all_gather x4, waiting for transfers between devices, global_gram(): total = jnp.sum(lax.all_gather(partial_gram, ('group', 'bulk')), axis=0)  229 us
    reduce_scatter x2, waiting for transfers between devices, operate(): owed = lax.psum_scatter(buffer, 'bulk', scatter_dimension=0, tiled=True)  148 us
    ppermute x5, waiting for transfers between devices, from_partner(): return lax.ppermute(value, axis, pairs)  80 us
    another operation x9, other arithmetic, chol_apply(): factor = jnp.linalg.cholesky(matrix)  23.9 us
    all_gather x2, blocking collectives, operate(): lax.all_gather(vectors[:boundary_rows], 'group', axis=0, tiled=True)  23.3 us
    another operation x6, other arithmetic, chol_apply(): lax.linalg.triangular_solve(factor, middle, left_side=True, lower=True, t...  22.2 us
    all_gather x2, waiting for transfers between devices, operate(): panel = lax.all_gather(vectors, 'bulk', axis=0, tiled=True)  19.9 us
    scatter-add x2, other arithmetic, operate(): jax.ops.segment_sum(flat_terms, column_ids.reshape(-1), num_segments=grou...  15.8 us
  transfers between devices with their start and end apart: 13, of which 12 were waited for; matrix products, arithmetic and copies ran while one was open for 16% of the time, Pallas kernels for 0%

profile of v1, /device:TPU:1, one launch (start us, length us, event | category | flops | bytes accessed | tf_op | source)
XLA Modules:
  0.0 714.1 jit_solution(12491313526976643210)
XLA Ops:
  7.3 1.9 copy.89
  9.9 1.6 copy.38
  12.1 2.6 scatter_custom_fusion.1
  15.9 1.5 gather_fusion
  18.7 2.2 gather_fusion.5
  25.3 3.1 fusion.4
  28.4 2.5 broadcast.320.clone
  30.9 8.0 %scatter_fusion = f32[128,64,128]{2,1,0:T(8,128)} fusion(f32[128,64,128]{2,1,0:T(8,128)} %broadcast.320.clone, s32[44]{0:T(128)} %reshape.516, f32[44,64,128]{2,1,0:T(8,128)} %bitcast.226), kind=kCustom, calls=%fused_computation.9 | custom fusion | flops 360448 | bytes 4325552 | tf_op jit(solution)/shard_map/scatter-add | solution.py:40
  41.1 13.2 %all_gather.37 = f32[8,64,128]{2,1,0:T(8,128)} all-gather(f32[2,64,128]{2,1,0:T(8,128)} %slice.208), channel_id=1, replica_groups=mesh['group'=4,'bulk'=32] {'group'}, dimensions={0}, use_global_device_ids=true | all-gather | bytes 327680 | tf_op jit(solution)/shard_map/all_gather | solution.py:33
  55.0 5.1 all-gather.11.cloned.1.call-done
  60.1 4.0 gather_fusion.1
  64.1 5.4 fusion.12
  69.5 73.9 %reduce-scatter.3.cloned.1.call-done = f32[4,64,128]{2,1,0:T(8,128)} async-done(((f32[128,64,128]{2,1,0:T(8,128)}), f32[4,64,128]{2,1,0:T(8,128)}) %reduce-scatter.3.cloned.1.call-update) | async-done | bytes 131088 | tf_op jit(solution)/shard_map/reduce_scatter | solution.py:41
  143.4 1.7 fusion.21
  145.1 1.6 fusion.29
  148.2 1.4 copy.40
  150.7 64.4 %all-gather.17.cloned.1.call-done = f32[8192,64]{1,0:T(8,128)} async-done(((f32[64,64]{1,0:T(8,128)}), f32[8192,64]{1,0:T(8,128)}) %all-gather.17.cloned.1.call-update) | async-done | bytes 2097168 | tf_op jit(solution)/shard_map/all_gather | solution.py:24
  215.1 3.1 reduce_sum.37
  218.2 1.4 copy.44
  219.6 1.4 fusion.56
  221.0 61.3 %all-gather.15.cloned.1.call-done = f32[8192,64]{1,0:T(8,128)} async-done(((f32[64,64]{1,0:T(8,128)}), f32[8192,64]{1,0:T(8,128)}) %all-gather.15.cloned.1.call-update) | async-done | bytes 2097168 | tf_op jit(solution)/shard_map/all_gather | solution.py:24
  282.3 3.1 reduce_sum.36
  285.4 1.4 copy.64
  286.9 1.4 fusion.61
  288.2 1.4 copy.43
  289.7 1.4 fusion.60
  291.1 7.2 %cholesky.59 = f32[64,64]{1,0:T(8,128)} custom-call(f32[64,64]{1,0:T(8,128)} %fusion.60), custom_call_target="Cholesky" | custom-call | tf_op jit(solution)/shard_map/jit(cholesky)/cholesky | solution.py:17
  299.8 2.1 fusion.36
  301.8 6.3 custom-call.13
  317.1 1.5 bitcast_dynamic-update-slice_fusion
  318.6 1.4 copy.47
  320.0 1.4 fusion.55
  321.4 7.2 %cholesky.70 = f32[64,64]{1,0:T(8,128)} custom-call(f32[64,64]{1,0:T(8,128)} %fusion.55), custom_call_target="Cholesky" | custom-call | tf_op jit(solution)/shard_map/jit(cholesky)/cholesky | solution.py:17
  330.1 2.1 fusion.37
  332.2 6.3 custom-call.15
  340.7 1.4 bitcast_dynamic-update-slice_fusion.2
  342.1 35.8 %all-gather.19.cloned.1.call-done = f32[8192,64]{1,0:T(8,128)} async-done(((f32[64,64]{1,0:T(8,128)}), f32[8192,64]{1,0:T(8,128)}) %all-gather.19.cloned.1.call-update) | async-done | bytes 2097168 | tf_op jit(solution)/shard_map/all_gather | solution.py:24
  377.9 3.1 reduce_sum.38
  381.0 1.4 copy.48
  390.4 2.2 broadcast_select_fusion
  392.6 21.3 %collective-permute-done.1 = f32[221184]{0:T(1024)} collective-permute-done((f32[221184]{0:T(1024)}, f32[221184]{0:T(1024)}, u32[]{:S(2)}, u32[]{:S(2)}) %collective-permute-start.1) | collective-permute-done | bytes 884768 | tf_op jit(solution)/shard_map/ppermute | solution.py:13
  413.9 2.2 broadcast_select_fusion.1
  417.3 20.8 %collective-permute-done.2 = f32[221184]{0:T(1024)} collective-permute-done((f32[221184]{0:T(1024)}, f32[221184]{0:T(1024)}, u32[]{:S(2)}, u32[]{:S(2)}) %collective-permute-start.2) | collective-permute-done | bytes 884768 | tf_op jit(solution)/shard_map/ppermute | solution.py:13
  438.1 2.2 broadcast_select_fusion.2
  440.3 19.6 %collective-permute-done.3 = f32[221184]{0:T(1024)} collective-permute-done((f32[221184]{0:T(1024)}, f32[221184]{0:T(1024)}, u32[]{:S(2)}, u32[]{:S(2)}) %collective-permute-start.3) | collective-permute-done | bytes 884768 | tf_op jit(solution)/shard_map/ppermute | solution.py:13
  459.9 2.2 broadcast_select_fusion.3
  464.0 18.3 %collective-permute-done.4 = f32[221184]{0:T(1024)} collective-permute-done((f32[221184]{0:T(1024)}, f32[221184]{0:T(1024)}, u32[]{:S(2)}, u32[]{:S(2)}) %collective-permute-start.4) | collective-permute-done | bytes 884768 | tf_op jit(solution)/shard_map/ppermute | solution.py:13
  484.5 2.0 fusion.40
  489.7 1.4 and_reduce_fusion
  493.7 3.2 fusion
  496.9 2.5 broadcast.320
  499.4 7.8 %scatter_fusion.1 = f32[128,64,128]{2,1,0:T(8,128)} fusion(f32[128,64,128]{2,1,0:T(8,128)} %broadcast.320, s32[44]{0:T(128)S(1)} %broadcast_subtract_fusion.1, f32[44,64,128]{2,1,0:T(8,128)} %bitcast.227), kind=kCustom, calls=%fused_computation.11 | custom fusion | flops 360448 | bytes 4325552 | tf_op jit(solution)/shard_map/scatter-add | solution.py:40
  507.5 10.1 %all_gather.45 = f32[8,64,128]{2,1,0:T(8,128)} all-gather(f32[2,64,128]{2,1,0:T(8,128)S(1)} %slice.243), channel_id=1, replica_groups=mesh['group'=4,'bulk'=32] {'group'}, dimensions={0}, use_global_device_ids=true | all-gather | bytes 327680 | tf_op jit(solution)/shard_map/all_gather | solution.py:33
  517.6 2.1 fusion.35
  519.7 14.8 %all-gather.13.cloned.1.call-done = f32[128,64,128]{2,1,0:T(8,128)} async-done(((f32[4,64,128]{2,1,0:T(8,128)}), f32[128,64,128]{2,1,0:T(8,128)}) %all-gather.13.cloned.1.call-update) | async-done | bytes 4194320 | tf_op jit(solution)/shard_map/all_gather | solution.py:39
  534.5 4.0 gather_fusion.7
  538.5 5.4 fusion.15
  543.9 73.9 %reduce-scatter.5.cloned.1.call-done = f32[4,64,128]{2,1,0:T(8,128)} async-done(((f32[128,64,128]{2,1,0:T(8,128)}), f32[4,64,128]{2,1,0:T(8,128)}) %reduce-scatter.5.cloned.1.call-update) | async-done | bytes 131088 | tf_op jit(solution)/shard_map/reduce_scatter | solution.py:41
  617.8 1.7 fusion.19
  619.5 1.6 fusion.27
  622.1 68.0 %all-gather.21.cloned.1.call-done = f32[8192,64]{1,0:T(8,128)} async-done(((f32[64,64]{1,0:T(8,128)}), f32[8192,64]{1,0:T(8,128)}) %all-gather.21.cloned.1.call-update) | async-done | bytes 2097168 | tf_op jit(solution)/shard_map/all_gather | solution.py:24
  690.1 2.5 reduce_sum.39
  692.8 5.8 cholesky.81
  700.0 4.9 custom-call.17
  (130 shorter events, 47.1 us)
Async XLA Ops:
  7.2 137.9 %copy-start = (f32[2,4,128,128]{3,2,1,0:T(8,128)S(1)}, f32[2,4,128,128]{3,2,1,0:T(8,128)}, u32[]{:S(2)}) copy-start(f32[2,4,128,128]{3,2,1,0:T(8,128)} %param.29) | copy-start | bytes 1572868
  7.2 18.1 %copy-start.3 = (f32[4,64,128]{2,1,0:T(8,128)S(1)}, f32[4,64,128]{2,1,0:T(8,128)}, u32[]{:S(2)}) copy-start(f32[4,64,128]{2,1,0:T(8,128)} %param.26) | copy-start | bytes 393220
  7.2 16.2 %copy-start.2 = (s32[512]{0:T(512)S(1)}, s32[512]{0:T(512)}, u32[]{:S(2)}) copy-start(s32[512]{0:T(512)} %param.31) | copy-start | bytes 6148
  7.2 4.3 copy-start.1
  7.2 52.9 %all-gather.11.cloned.1.call-start = ((), (), s32[]{:S(2)}) async-start(), calls=%async_computation.2 | async-start | bytes 4325376 | tf_op jit(solution)/shard_map/all_gather | solution.py:39
  7.3 1.9 copy-start.17
  9.9 133.5 %reduce-scatter.3.cloned.1.call-start = ((), (), s32[]{:S(2)}) async-start(), calls=%async_computation.3 | async-start | bytes 4325376 | tf_op jit(solution)/shard_map/reduce_scatter | solution.py:41
  14.7 16.1 %copy-start.18 = (s32[1024]{0:T(1024)}, s32[1024]{0:T(1024)S(1)}, u32[]{:S(2)}) copy-start(s32[1024]{0:T(1024)S(1)} %pad_clamp_fusion.4) | copy-start | bytes 12292
  38.8 1.7 copy-start.20
  38.9 176.2 %all-gather.17.cloned.1.call-start = ((), (), s32[]{:S(2)}) async-start(), calls=%async_computation.7 | async-start | bytes 4227072 | tf_op jit(solution)/shard_map/all_gather | solution.py:24
  39.8 242.5 %all-gather.15.cloned.1.call-start = ((), (), s32[]{:S(2)}) async-start(), calls=%async_computation.6 | async-start | bytes 4227072 | tf_op jit(solution)/shard_map/all_gather | solution.py:24
  146.7 0.7 copy-start.9
  149.7 228.2 %all-gather.19.cloned.1.call-start = ((), (), s32[]{:S(2)}) async-start(), calls=%async_computation.8 | async-start | bytes 4227072 | tf_op jit(solution)/shard_map/all_gather | solution.py:24
  310.1 0.6 copy-start.15
  311.9 0.7 copy-start.6
  313.5 221.0 %all-gather.13.cloned.1.call-start = ((), (), s32[]{:S(2)}) async-start(), calls=%async_computation.4 | async-start | bytes 4325376 | tf_op jit(solution)/shard_map/all_gather | solution.py:39
  339.5 0.6 copy-start.10
  385.7 0.7 copy-start.4
  386.9 3.5 collective-permute-start
  392.6 21.3 %collective-permute-start.1 = (f32[221184]{0:T(1024)}, f32[221184]{0:T(1024)}, u32[]{:S(2)}, u32[]{:S(2)}) collective-permute-start(f32[221184]{0:T(1024)} %broadcast_select_fusion), channel_id=1, source_target_pairs={{0,2},{1,3},{2,0},{3,1},{4,6},{5,7},{6,4},{7,5},{8,10},{9,11},{10,... | collective-permute-start | bytes 2654216 | tf_op jit(solution)/shard_map/ppermute | solution.py:13
  416.1 47.1 %copy-start.21 = (s32[3]{0:T(128)S(1)}, s32[3]{0:T(128)}, u32[]{:S(2)}) copy-start(s32[3]{0:T(128)} %constant.238.clone.1) | copy-start | bytes 40
  416.1 47.9 %copy-start.11 = (f32[64,4,128]{2,0,1:T(8,128)S(1)}, f32[64,4,128]{2,0,1:T(8,128)}, u32[]{:S(2)}) copy-start(f32[64,4,128]{2,0,1:T(8,128)} %copy-done.10) | copy-start | bytes 393220
  416.1 22.0 %collective-permute-start.2 = (f32[221184]{0:T(1024)}, f32[221184]{0:T(1024)}, u32[]{:S(2)}, u32[]{:S(2)}) collective-permute-start(f32[221184]{0:T(1024)} %broadcast_select_fusion.1), channel_id=1, source_target_pairs={{0,4},{1,5},{2,6},{3,7},{4,0},{5,1},{6,2},{7,3},{8,12},{9,13},{10,... | collective-permute-start | bytes 2654216 | tf_op jit(solution)/shard_map/ppermute | solution.py:13
  440.3 19.6 %collective-permute-start.3 = (f32[221184]{0:T(1024)}, f32[221184]{0:T(1024)}, u32[]{:S(2)}, u32[]{:S(2)}) collective-permute-start(f32[221184]{0:T(1024)} %broadcast_select_fusion.2), channel_id=1, source_target_pairs={{0,8},{1,9},{2,10},{3,11},{4,12},{5,13},{6,14},{7,15},{8,0},{9,1},... | collective-permute-start | bytes 2654216 | tf_op jit(solution)/shard_map/ppermute | solution.py:13
  440.3 48.5 %copy-start.19 = (s32[4,11,1]{1,0,2:T(4,128)S(1)}, s32[4,11,1]{1,0,2:T(4,128)}, u32[]{:S(2)}) copy-start(s32[4,11,1]{1,0,2:T(4,128)} %get-tuple-element.96) | copy-start | bytes 532
  462.1 20.2 %collective-permute-start.4 = (f32[221184]{0:T(1024)}, f32[221184]{0:T(1024)}, u32[]{:S(2)}, u32[]{:S(2)}) collective-permute-start(f32[221184]{0:T(1024)} %broadcast_select_fusion.3), channel_id=1, source_target_pairs={{0,16},{1,17},{2,18},{3,19},{4,20},{5,21},{6,22},{7,23},{8,24},{9,... | collective-permute-start | bytes 2654216 | tf_op jit(solution)/shard_map/ppermute | solution.py:13
  483.6 0.9 copy-start.8
  486.6 0.6 copy-start.13
  487.2 130.6 %reduce-scatter.5.cloned.1.call-start = ((), (), s32[]{:S(2)}) async-start(), calls=%async_computation.5 | async-start | bytes 4325376 | tf_op jit(solution)/shard_map/reduce_scatter | solution.py:41
  488.8 4.9 copy-start.5
  507.2 182.9 %all-gather.21.cloned.1.call-start = ((), (), s32[]{:S(2)}) async-start(), calls=%async_computation.9 | async-start | bytes 4227072 | tf_op jit(solution)/shard_map/all_gather | solution.py:24
  619.5 85.5 %copy-start.12 = (f32[64,64]{1,0:T(8,128)S(1)}, f32[64,64]{1,0:T(8,128)}, u32[]{:S(2)}) copy-start(f32[64,64]{1,0:T(8,128)} %reduce_sum.38) | copy-start | bytes 49156
  619.5 85.5 %copy-start.16 = (f32[64,64]{0,1:T(8,128)S(1)}, f32[64,64]{0,1:T(8,128)}, u32[]{:S(2)}) copy-start(f32[64,64]{0,1:T(8,128)} %copy.48) | copy-start | bytes 49156
  619.5 85.9 %copy-start.7 = (f32[4,64,128]{2,1,0:T(8,128)S(1)}, f32[4,64,128]{2,1,0:T(8,128)}, u32[]{:S(2)}) copy-start(f32[4,64,128]{2,1,0:T(8,128)} %get-tuple-element.93) | copy-start | bytes 393220
  621.2 85.2 %copy-start.14 = (f32[4,64,128]{2,1,0:T(8,128)S(1)}, f32[4,64,128]{2,1,0:T(8,128)}, u32[]{:S(2)}) copy-start(f32[4,64,128]{2,1,0:T(8,128)} %copy-done.13) | copy-start | bytes 393220
Sparse Core Ops, SparseCore 0:
  10.3 49.7 all-gather.10
  63.7 79.6 reduce-scatter.2
  147.2 67.8 all-gather.16
  218.1 64.1 all-gather.14
  313.6 64.2 all-gather.18
  487.4 47.0 all-gather.12
  538.1 79.6 reduce-scatter.4
  622.2 67.8 all-gather.20
